TPU v7x, 32 devices: a whole 2x2x4 slice. The times are simulated.
32 devices in a mesh: dom: 8 (over z, y), grp: 4 (over x, core).
Axes of the slice: x: 2, y: 2, z: 4, core: 2. Of those that a mesh axis runs over, the one named last changes fastest.
Arguments:
- profile: bfloat16 [768, 2, 64, 128], P(('dom', 'grp')), may hold values from -6 to 6
- forcing: bfloat16 [768, 2, 128], P(('dom', 'grp')), may hold values from -6 to 6
- height: bfloat16 [768, 128], P(('dom', 'grp')), may hold values from 0.5 to 2
- area: float32 [768, 128], P(('dom', 'grp')), may hold values from 0.5 to 2
- stretch: int32 [768], P(('dom', 'grp')), may hold values from 0 to 3
- face_cell: int32 [768, 128], P(('dom', 'grp')), may hold values from 0 to 127
- match_owner: int32 [8, 4, 24], P(None, 'grp'), may hold values from 0 to 7, as said below
- match_block: int32 [8, 4, 24], P(None, 'grp'), may hold values from 0 to 11
- live_blocks: int32 [32], replicated, may hold values from 6 to 24, as said below
- cell_velocity: bfloat16 [384, 2, 128], P(('dom', 'grp')), may hold values from -6 to 6
Outputs:
- wall_shear: float32 [768, 2, 128], P(('dom', 'grp'))
- wall_force: float32 [384, 2, 128], P(('dom', 'grp'))
Inputs may be any that keep to these rules, and one draw needn't show every extreme that they name: `match_owner`: of the blocks of one device, at most 6 have the same owner, and in every device one owner has exactly 6. The first live_blocks blocks of a device hold faces. Among the devices of one dom index, exactly one has all 24 blocks in use.
All inputs are finite; a program needn't handle non-finite values.
Results may differ from a plain program's by a relative error of at most 0.001.
Values may be sent and summed in bfloat16 or wider, within the bound.
A program may use at most 64 MiB of HBM per device.

v0:
```python
import jax
import jax.numpy as jnp
from jax import lax
from jax.sharding import PartitionSpec as P

STEPS = 4


VISCOSITY = 0.005
KARMAN = 0.41
TIME_STEP = 2.0
PUSH_GAIN = 0.5
BASE_RATE = 1.5


def wall_grid(height, stretch, points):
    levels = jnp.arange(points + 1, dtype=jnp.float32) / points
    stretch_rate = BASE_RATE + stretch.astype(jnp.float32)
    growth = jnp.exp(stretch_rate[:, None] * levels[None, :]) - 1.0
    fraction = growth / growth[:, -1:]
    depths = fraction[:, :, None] * height.astype(jnp.float32)[:, None, :]
    spacing = depths[:, 1:] - depths[:, :-1]
    middle = 0.5 * (depths[:, 1:] + depths[:, :-1])
    return (spacing, middle)


def viscosity(profile_now, spacing, middle):
    below_point = jnp.concatenate(
        [jnp.zeros_like(profile_now[:, :, :1]), profile_now[:, :, :-1]], axis=2
    )
    increment = profile_now - below_point
    strain = jnp.sqrt(increment[:, 0] ** 2 + increment[:, 1] ** 2) / spacing
    return VISCOSITY + (KARMAN * middle) ** 2 * strain


def thomas_solve(lower_band, diagonal, upper_band, right_side):
    points = diagonal.shape[1]
    factor_list = []
    value_list = []
    denom = diagonal[:, 0]
    factor_now = upper_band[:, 0] / denom
    value_now = right_side[:, :, 0] / denom[:, None]
    factor_list.append(factor_now)
    value_list.append(value_now)
    for level in range(1, points):
        lower_now = lower_band[:, level]
        denom = diagonal[:, level] - lower_now * factor_now
        factor_now = upper_band[:, level] / denom
        value_now = (right_side[:, :, level] - lower_now[:, None] * value_now) / denom[:, None]
        factor_list.append(factor_now)
        value_list.append(value_now)
    answer = [None] * points
    answer[points - 1] = value_list[points - 1]
    for level in range(points - 2, -1, -1):
        answer[level] = value_list[level] - factor_list[level][:, None] * answer[level + 1]
    return jnp.stack(answer, axis=2)


def implicit_step(profile_now, source, matching, spacing, middle):
    points = spacing.shape[1]
    mixing = viscosity(profile_now, spacing, middle)
    upper_mix = jnp.concatenate([mixing[:, 1:], mixing[:, -1:]], axis=1)
    upper_gap = jnp.concatenate([spacing[:, 1:], spacing[:, -1:]], axis=1)
    centre = 0.5 * (spacing + upper_gap)
    down_coef = TIME_STEP * mixing / (spacing * centre)
    up_coef = TIME_STEP * upper_mix / (upper_gap * centre)
    row_index = lax.broadcasted_iota(jnp.int32, spacing.shape, 1)
    last_row = row_index == points - 1
    lower_band = jnp.where((row_index == 0) | last_row, 0.0, -down_coef)
    upper_band = jnp.where(last_row, 0.0, -up_coef)
    diagonal = jnp.where(last_row, 1.0, 1.0 + down_coef + up_coef)
    right_side = jnp.where(
        last_row[:, None], matching[:, :, None, :], profile_now + TIME_STEP * source[:, :, None, :]
    )
    return thomas_solve(lower_band, diagonal, upper_band, right_side)


def wall_shear_of(profile_in, forcing, matching, height, stretch):
    points = profile_in.shape[2]
    spacing, middle = wall_grid(height, stretch, points)
    start_profile = profile_in.astype(jnp.float32)
    matching = matching.astype(jnp.float32)
    source = PUSH_GAIN * (forcing.astype(jnp.float32) + matching - start_profile[:, :, -1, :])
    profile_now = jnp.concatenate([start_profile[:, :, :-1], matching[:, :, None, :]], axis=2)
    for inner_step in range(STEPS):
        profile_now = implicit_step(profile_now, source, matching, spacing, middle)
    mixing = viscosity(profile_now, spacing, middle)
    return (mixing[:, 0] / spacing[:, 0])[:, None, :] * profile_now[:, :, 0]


def solve_tiles(members, live_count, tile_size):
    row_total = members[0].shape[0]
    face_count = members[0].shape[-1]

    def advance(tile_index, result):
        first_row = tile_index * tile_size
        pieces = [lax.dynamic_slice_in_dim(member, first_row, tile_size, 0) for member in members]
        shear_tile = wall_shear_of(pieces[0], pieces[1], pieces[2], pieces[3], pieces[4])
        positions = first_row + jnp.arange(tile_size, dtype=jnp.int32)
        shear_tile = jnp.where((positions < live_count)[:, None, None], shear_tile, 0.0)
        return lax.dynamic_update_slice_in_dim(result, shear_tile, first_row, 0)

    blank_rows = jnp.zeros((row_total, 2, face_count), jnp.float32)
    return lax.fori_loop(0, (live_count + tile_size - 1) // tile_size, advance, blank_rows)


def body(
    profile,
    forcing,
    height,
    area,
    stretch,
    face_cell,
    match_owner,
    match_block,
    live_blocks,
    cell_velocity,
):
    dom_count = lax.axis_size("dom")
    grp_count = lax.axis_size("grp")
    dom_index = lax.axis_index("dom")
    grp_index = lax.axis_index("grp")
    blocks = profile.shape[0]
    face_count = profile.shape[3]
    capacity = max(2, 2 * blocks // dom_count)
    owners = match_owner[:, 0, :]
    targets = match_block[:, 0, :]
    block_ids = jnp.arange(blocks, dtype=jnp.int32)
    same_owner = owners[:, :, None] == owners[:, None, :]
    earlier = block_ids[None, :] < block_ids[:, None]
    owner_rank = jnp.sum((same_owner & earlier[None]).astype(jnp.int32), axis=2)
    owned_here = owners == dom_index
    slot_ids = jnp.arange(capacity, dtype=jnp.int32)
    chosen = owned_here[:, None, :] & (owner_rank[:, None, :] == slot_ids[None, :, None])
    slot_block = jnp.sum(jnp.where(chosen, targets[:, None, :], 0), axis=2)
    filled = jnp.any(chosen, axis=2)
    outgoing = jnp.take(cell_velocity, slot_block.reshape(-1), axis=0).reshape(
        dom_count, capacity, 2, face_count
    )
    incoming = lax.all_to_all(outgoing, "dom", split_axis=0, concat_axis=0, tiled=True)
    my_owner = lax.dynamic_index_in_dim(owners, dom_index, 0, keepdims=False)
    my_rank = lax.dynamic_index_in_dim(owner_rank, dom_index, 0, keepdims=False)
    slot_index = my_owner * capacity + my_rank
    slot_rows = jnp.take(incoming.reshape(dom_count * capacity, 2, face_count), slot_index, axis=0)
    matching = jnp.take_along_axis(
        slot_rows, jnp.broadcast_to(face_cell[:, None, :], slot_rows.shape), axis=2
    )
    group_live = lax.dynamic_slice_in_dim(live_blocks, dom_index * grp_count, grp_count)
    own_live = jnp.sum(
        jnp.where(jnp.arange(grp_count, dtype=jnp.int32) == grp_index, group_live, 0)
    )
    shear_all = solve_tiles((profile, forcing, matching, height, stretch), own_live, 4)
    contrib = shear_all * area[:, None, :]
    cell_pick = (
        face_cell[:, :, None] == jnp.arange(face_count, dtype=jnp.int32)[None, None, :]
    ).astype(jnp.float32)
    per_cell = jnp.einsum("bcf,bfk->bck", contrib, cell_pick, precision=lax.Precision.HIGHEST)
    slot_pick = (
        slot_index[None, :] == jnp.arange(dom_count * capacity, dtype=jnp.int32)[:, None]
    ).astype(jnp.float32)
    packed_force = jnp.dot(
        slot_pick, per_cell.reshape(blocks, 2 * face_count), precision=lax.Precision.HIGHEST
    )
    force_rows = lax.all_to_all(
        packed_force.reshape(dom_count, capacity, 2 * face_count),
        "dom",
        split_axis=0,
        concat_axis=0,
        tiled=True,
    )
    cell_count = cell_velocity.shape[0]
    gather_pick = (
        filled.reshape(-1)[None, :]
        & (slot_block.reshape(-1)[None, :] == jnp.arange(cell_count, dtype=jnp.int32)[:, None])
    ).astype(jnp.float32)
    wall_force = jnp.dot(
        gather_pick,
        force_rows.reshape(dom_count * capacity, 2 * face_count),
        precision=lax.Precision.HIGHEST,
    )
    return (shear_all, wall_force.reshape(cell_count, 2, face_count))


def solution(mesh):
    in_specs = (
        P(("dom", "grp"), None, None, None),
        P(("dom", "grp"), None, None),
        P(("dom", "grp"), None),
        P(("dom", "grp"), None),
        P(("dom", "grp")),
        P(("dom", "grp"), None),
        P(None, "grp", None),
        P(None, "grp", None),
        P(),
        P(("dom", "grp"), None, None),
    )
    out_specs = (P(("dom", "grp"), None, None), P(("dom", "grp"), None, None))
    return jax.shard_map(body, mesh=mesh, in_specs=in_specs, out_specs=out_specs, check_vma=False)
```

profile of v0, /device:TPU:0, one launch (start us, length us, event | category | flops | bytes accessed | tf_op | source)
XLA Modules:
  0.0 221.0 jit_solution(17359444365223254850)
XLA Ops:
  0.7 0.7 broadcast_compare_fusion.2
  1.4 1.0 convert_reduce_fusion
  2.4 0.9 select_reduce_fusion
  4.2 0.7 broadcast_select_fusion
  4.9 7.3 %all-to-all-start = ((bf16[8,6,2,128]{3,2,1,0:T(2,128)(2,1)}), bf16[8,6,2,128]{3,2,1,0:T(2,128)(2,1)S(1)}, u32[]{:S(2)}, u32[]{:S(2)}) async-start(bf16[8,6,2,128]{3,2,1,0:T(2,128)(2,1)} %broadcast_select_fusion), calls=%async_computation | async-start | bytes 49152 | tf_op jit(solution)/shard_map/all_to_all | solution.py:140
  13.6 0.7 broadcast_compare_fusion.1
  14.3 0.7 broadcast_add_fusion
  15.1 0.7 shift-left_or_fusion
  16.5 1.4 fusion.1265
  19.6 54.6 %gather_fusion.2 = bf16[6144]{0:T(1024)(128)(2,1)S(1)} fusion(bf16[24,2,128]{2,1,0:T(2,128)(2,1)S(1)} %broadcast_select_fusion.1, s32[6144]{0:T(1024)S(1)} %bitcast.11214), kind=kCustom, calls=%fused_computation.2 | custom fusion | bytes 98304 | tf_op jit(solution)/shard_map/jit(take_along_axis)/gather | solution.py:145
  74.4 66.5 %while.10 = (s32[]{:T(128)}, f32[24,2,128]{2,1,0:T(2,128)S(1)}, s32[]{:T(128)}, s32[]{:T(128)}, s32[24]{0:T(128)S(1)}, /*index=5*/bf16[24,128]{1,0:T(8,128)(2,1)...) while((s32[]{:T(128)}, f32[24,2,128]{2,1,0:T(2,128)S(1)}, ...), condition=%wide.region_4.5_spmd, body=%wide.region_3.4_spmd.sunk | while | flops 8349287 | bytes 35359956 | solution.py:104
  75.5 0.7 fusion.1670
  76.2 0.7 constant_dynamic-slice_fusion.7
  77.2 0.9 constant_dynamic-slice_fusion.8
  80.9 0.7 constant_dynamic-update-slice_fusion.834
  85.1 0.7 constant_dynamic-update-slice_fusion.900
  89.3 0.7 constant_dynamic-update-slice_fusion.966
  93.5 0.7 constant_dynamic-update-slice_fusion.1032
  97.7 0.7 fusion.1670
  98.4 0.7 constant_dynamic-slice_fusion.7
  99.4 0.9 constant_dynamic-slice_fusion.8
  111.4 0.7 constant_dynamic-update-slice_fusion.966
  115.6 0.7 constant_dynamic-update-slice_fusion.1032
  119.8 0.7 fusion.1670
  120.5 0.7 constant_dynamic-slice_fusion.7
  121.5 0.9 constant_dynamic-slice_fusion.8
  133.6 0.7 constant_dynamic-update-slice_fusion.966
  137.8 0.7 constant_dynamic-update-slice_fusion.1032
  140.8 1.2 fusion.1249
  142.1 0.8 fusion.1254
  142.9 70.5 %all-to-all-start.1 = ((f32[8,6,256]{2,1,0:T(8,128)}), f32[8,6,256]{2,1,0:T(8,128)S(1)}, u32[]{:S(2)}, u32[]{:S(2)}) async-start(f32[8,6,256]{2,1,0:T(8,128)} %fusion.1254), calls=%async_computation.1 | async-start | bytes 131072 | tf_op jit(solution)/shard_map/all_to_all | solution.py:164
  213.7 6.5 %all-to-all-done.1 = f32[8,6,256]{2,1,0:T(8,128)S(1)} async-done(((f32[8,6,256]{2,1,0:T(8,128)}), f32[8,6,256]{2,1,0:T(8,128)S(1)}, u32[]{:S(2)}, u32[]{:S(2)}) %all-to-all-start.1) | async-done | bytes 49184 | tf_op jit(solution)/shard_map/all_to_all | solution.py:164
  (1323 shorter events, 53.9 us)
Async XLA Ops:
  0.6 3.0 %copy-start = (bf16[12,2,128]{2,1,0:T(2,128)(2,1)S(1)}, bf16[12,2,128]{2,1,0:T(2,128)(2,1)}, u32[]{:S(2)}) copy-start(bf16[12,2,128]{2,1,0:T(2,128)(2,1)} %param.21) | copy-start | bytes 18436
  4.9 13.9 %all-to-all-start = ((bf16[8,6,2,128]{3,2,1,0:T(2,128)(2,1)}), bf16[8,6,2,128]{3,2,1,0:T(2,128)(2,1)S(1)}, u32[]{:S(2)}, u32[]{:S(2)}) async-start(bf16[8,6,2,128]{3,2,1,0:T(2,128)(2,1)} %broadcast_select_fusion), calls=%async_computation | async-start | bytes 49152 | tf_op jit(solution)/shard_map/all_to_all | solution.py:140
  19.6 54.7 %copy-start.1 = (s32[24,128]{1,0:T(8,128)S(1)}, s32[24,128]{1,0:T(8,128)}, u32[]{:S(2)}) copy-start(s32[24,128]{1,0:T(8,128)} %param.17) | copy-start | bytes 36868
  19.6 54.7 %copy-start.4 = (s32[24]{0:T(128)S(1)}, s32[24]{0:T(128)}, u32[]{:S(2)}) copy-start(s32[24]{0:T(128)} %param.16) | copy-start | bytes 292
  74.3 66.5 %copy-start.3 = (f32[24,128]{1,0:T(8,128)S(1)}, f32[24,128]{1,0:T(8,128)}, u32[]{:S(2)}) copy-start(f32[24,128]{1,0:T(8,128)} %param.15) | copy-start | bytes 36868
  140.8 80.2 %copy-start.2 = (f32[24,2,128]{2,1,0:T(2,128)}, f32[24,2,128]{2,1,0:T(2,128)S(1)}, u32[]{:S(2)}) copy-start(f32[24,2,128]{2,1,0:T(2,128)S(1)} %get-tuple-element.126) | copy-start | bytes 73732
  142.9 77.4 %all-to-all-start.1 = ((f32[8,6,256]{2,1,0:T(8,128)}), f32[8,6,256]{2,1,0:T(8,128)S(1)}, u32[]{:S(2)}, u32[]{:S(2)}) async-start(f32[8,6,256]{2,1,0:T(8,128)} %fusion.1254), calls=%async_computation.1 | async-start | bytes 131072 | tf_op jit(solution)/shard_map/all_to_all | solution.py:164
where the time goes:
time: 222 us; the launch traced here: 221 us
  starting transfers between devices  77.8 us (35%)
  local copies, waits for them, and re-layouts  72.6 us (33%)
  other arithmetic  55 us (25%)
  waiting for transfers between devices  6.71 us (3%)
  loops' own time  5.29 us (2%)
    all_to_all x1, starting transfers between devices, body(): lax.all_to_all(packed_force.reshape(dom_count, capacity, 2 * face_count),...  70.5 us
    gather x1, local copies, waits for them, and re-layouts, body(): jnp.take_along_axis(slot_rows, jnp.broadcast_to(face_cell[:, None, :], sl...  54.6 us
    div x132, other arithmetic, thomas_solve(): (right_side[:, :, level] - lower_now[:, None] * value_now) / denom[:, None]  11.6 us
    while x33, other arithmetic  10.6 us
    while x918, local copies, waits for them, and re-layouts  9.17 us
    all_to_all x1, starting transfers between devices, body(): lax.all_to_all(outgoing, 'dom', split_axis=0, concat_axis=0, tiled=True)  7.31 us
    sub x12, other arithmetic, thomas_solve(): denom = diagonal[:, level] - lower_now * factor_now  6.81 us
    all_to_all x1, waiting for transfers between devices, body(): lax.all_to_all(packed_force.reshape(dom_count, capacity, 2 * face_count),...  6.54 us
  transfers between devices with their start and end apart: 2, of which 2 were waited for; matrix products, arithmetic and copies ran while one was open for 3% of the time, Pallas kernels for 0%

commit v1 on v0

v1 whole, which is shorter than its diff:
```python
import functools

import jax
import jax.numpy as jnp
from jax import lax
from jax.experimental import pallas as pl
from jax.experimental.pallas import tpu as pltpu
from jax.sharding import PartitionSpec as P

STEPS = 4
VISCOSITY = 0.005
KARMAN = 0.41
TIME_STEP = 2.0
PUSH_GAIN = 0.5
BASE_RATE = 1.5
MESH = pl.DeviceIdType.MESH
F32 = jnp.float32
BF16 = jnp.bfloat16


def kernel(
    doms,
    grps,
    prof_h,
    forc_h,
    height_h,
    area_h,
    stretch_h,
    face_h,
    owner_h,
    target_h,
    live_h,
    cell_h,
    shear_ref,
    force_ref,
    prof,
    forc,
    height,
    area,
    stretch,
    face,
    owner,
    target,
    live,
    table,
    stage,
    u,
    gval,
    fac,
    base,
    quad,
    gap,
    pick,
    cells,
    packed,
    arrived,
    in_sem,
    own_sem,
    cell_send,
    cell_recv,
    force_send,
    force_recv,
):
    blocks, _, points, faces = prof.shape
    rows = cell_h.shape[0]
    me = lax.axis_index("dom")
    mine = lax.axis_index("grp")
    wide = (blocks, faces)

    barrier = pltpu.get_barrier_semaphore()
    for j in range(1, doms):
        pl.semaphore_signal(
            barrier, inc=1, device_id={"dom": lax.rem(me + j, doms)}, device_id_type=MESH
        )
    loads = []
    for i, (src, dst) in enumerate(
        (
            (stretch_h, stretch),
            (height_h, height),
            (owner_h, owner),
            (target_h, target),
            (face_h, face),
            (prof_h, prof),
            (forc_h, forc),
            (area_h, area),
            (live_h, live),
        )
    ):
        loads.append(pltpu.make_async_copy(src, dst, in_sem.at[i]))
        loads[-1].start()
    own = pltpu.make_async_copy(cell_h, table.at[me], own_sem)
    own.start()
    pl.semaphore_wait(barrier, doms - 1)
    cell_copies = []
    for j in range(1, doms):
        cell_copies.append(
            pltpu.make_async_remote_copy(
                src_ref=cell_h,
                dst_ref=table.at[me],
                send_sem=cell_send.at[j],
                recv_sem=cell_recv.at[j],
                device_id={"dom": lax.rem(me + j, doms)},
                device_id_type=MESH,
            )
        )
        cell_copies[-1].start()
    for load in loads:
        load.wait()

    eye = lax.broadcasted_iota(jnp.int32, (blocks, blocks), 0) == lax.broadcasted_iota(
        jnp.int32, (blocks, blocks), 1
    )

    def as_column(row):
        spread = jnp.broadcast_to(row.astype(F32), (blocks, blocks))
        return jnp.sum(jnp.where(eye, spread, 0.0), axis=1, keepdims=True)

    rate = BASE_RATE + as_column(stretch[...])
    tall = height[...].astype(F32)
    step_rate = jnp.broadcast_to(rate / points, wide)
    growth = jnp.exp(step_rate)
    first = (growth - 1.0) / (jnp.exp(jnp.broadcast_to(rate, wide)) - 1.0)
    base_scale = TIME_STEP * VISCOSITY / (first * tall)
    gap_scale = 0.5 * tall * first * (1.0 + growth)
    mid_scale = 1.0 / (growth - 1.0)
    mid_first = 0.5 * (1.0 + growth)

    def grid_level(m, carry):
        level = m.astype(F32)
        shrink = jnp.exp(-step_rate * level)
        base[m] = base_scale * shrink
        ratio = KARMAN * (mid_first - shrink) * mid_scale
        quad[m] = TIME_STEP * ratio * ratio
        gap[m] = gap_scale * jnp.exp(step_rate * (level - 1.0))
        return carry

    lax.fori_loop(0, points, grid_level, 0)

    def widen(b, carry):
        stage[pl.ds(pl.multiple_of(b * 2 * points, 2 * points), 2 * points), :] = (
            prof[b].astype(F32).reshape(2 * points, faces)
        )
        return carry

    lax.fori_loop(0, blocks, widen, 0)

    def turn(k, carry):
        for c in range(2):
            u[k, c] = stage[pl.ds(c * points + k, blocks, stride=2 * points), :]
        return carry

    lax.fori_loop(0, points, turn, 0)

    face_now = face[...]
    cell_ids = lax.broadcasted_iota(jnp.int32, (faces, faces), 0)

    for b in range(blocks):
        pick[b] = (cell_ids == face_now[b : b + 1, :]).astype(F32).astype(BF16)

    row_global = owner[me] * rows + 2 * target[me]
    col_global = as_column(row_global).astype(jnp.int32)
    slots = doms * rows
    slot_lane = lax.broadcasted_iota(jnp.int32, (blocks, slots), 1)
    choose = jnp.concatenate(
        [(slot_lane == col_global + c).astype(F32) for c in range(2)], axis=0
    ).astype(BF16)

    own.wait()
    for copy in cell_copies:
        copy.wait()

    held = table[...].astype(F32).reshape(slots, faces).astype(BF16)
    slot_rows = jnp.dot(choose, held, preferred_element_type=F32)
    matching = [
        jnp.take_along_axis(
            slot_rows[c * blocks : (c + 1) * blocks], face_now, axis=1, mode="promise_in_bounds"
        )
        for c in range(2)
    ]
    source = []
    for c in range(2):
        push = forc[pl.ds(c, blocks, stride=2), :] + matching[c] - u[points - 1, c]
        source.append(TIME_STEP * PUSH_GAIN * push)
        u[points - 1, c] = matching[c]

    def flux(m, low, high):
        d0 = high[0] - low[0]
        d1 = high[1] - low[1]
        square = d0 * d0 + d1 * d1
        root = square * lax.rsqrt(jnp.maximum(square, 1e-37))
        return base[m] + quad[m] * root

    def point(k):
        return (u[k - 1, 0], u[k - 1, 1])

    zero = jnp.zeros(wide, F32)
    half = points // 2

    def eliminate(k, e, g, near, far, here):
        h = gap[k]
        p = h + near * e
        r = 1.0 / (p + far)
        e_new = p * r
        f_new = far * r
        g_new = tuple((h * (here[c] + source[c]) + near * g[c]) * r for c in range(2))
        return e_new, f_new, g_new

    def time_step(_, carry):
        below = point(1)
        low_flux = flux(0, (zero, zero), below)
        low_e, low_g = jnp.ones(wide, F32), (zero, zero)
        above = point(points - 1)
        edge = point(points)
        high_flux = flux(points - 1, above, edge)
        high_e, high_g = jnp.ones(wide, F32), edge
        for i in range(half):
            k = i + 1
            after = point(k + 1)
            next_flux = flux(k, below, after)
            low_e, low_f, low_g = eliminate(k, low_e, low_g, low_flux, next_flux, below)
            if i < half - 1:
                fac[k] = low_f
                for c in range(2):
                    gval[k, c] = low_g[c]
            low_flux, below = next_flux, after
            k = points - 1 - i
            if k > half:
                after = point(k - 1)
                next_flux = flux(k - 1, after, above)
                high_e, high_f, high_g = eliminate(
                    k, high_e, high_g, high_flux, next_flux, above
                )
                if k > half + 1:
                    fac[k] = high_f
                    for c in range(2):
                        gval[k, c] = high_g[c]
                high_flux, above = next_flux, after
        share = 1.0 / (low_e + low_f * high_e)
        down = [(low_g[c] + low_f * high_g[c]) * share for c in range(2)]
        up = [high_g[c] + high_f * down[c] for c in range(2)]
        for c in range(2):
            u[half - 1, c] = down[c]
            u[half, c] = up[c]
        for i in range(1, half):
            k = half - i
            f = fac[k]
            for c in range(2):
                down[c] = gval[k, c] + f * down[c]
                u[k - 1, c] = down[c]
            k = half + 1 + i
            if k < points:
                f = fac[k]
                for c in range(2):
                    up[c] = gval[k, c] + f * up[c]
                    u[k - 1, c] = up[c]
        return carry

    lax.fori_loop(0, STEPS, time_step, 0)

    wall = point(1)
    wall_flux = flux(0, (zero, zero), wall) * (1.0 / TIME_STEP)
    lane = lax.broadcasted_iota(jnp.int32, live.shape, 1)
    own_live = jnp.sum(
        jnp.where(lane == me * grps + mine, live[...], 0).astype(F32), axis=1, keepdims=True
    )
    alive = lax.broadcasted_iota(jnp.int32, wide, 0).astype(F32) < own_live
    size = area[...]
    pieces = []
    for c in range(2):
        shear = jnp.where(alive, wall_flux * wall[c], 0.0)
        shear_ref[pl.ds(c, blocks, stride=2), :] = shear
        pieces.append(shear * size)
    for c in range(2):
        top = pieces[c].astype(BF16).astype(F32)
        cells[pl.ds(c, blocks, stride=8), :] = top
        cells[pl.ds(2 + c, blocks, stride=8), :] = pieces[c] - top
    for c in range(4):
        cells[pl.ds(4 + c, blocks, stride=8), :] = zero
    for b in range(blocks):
        part = cells[pl.ds(8 * b, 8), :].astype(BF16)
        cells[pl.ds(8 * b, 8), :] = lax.dot_general(
            part, pick[b], (((1,), (1,)), ((), ())), preferred_element_type=F32
        )
    slot_row = lax.broadcasted_iota(jnp.int32, (slots, blocks), 0)
    total = jnp.zeros((slots, faces), F32)
    for c in range(2):
        by_cell = cells[pl.ds(c, blocks, stride=8), :] + cells[pl.ds(2 + c, blocks, stride=8), :]
        place = (slot_row == row_global + c).astype(F32)
        total += jnp.dot(
            place, by_cell, precision=lax.Precision.HIGHEST, preferred_element_type=F32
        )
    packed[...] = total.reshape(doms, rows, faces)
    force_copies = []
    for j in range(1, doms):
        peer = lax.rem(me + j, doms)
        force_copies.append(
            pltpu.make_async_remote_copy(
                src_ref=packed.at[peer],
                dst_ref=arrived.at[j],
                send_sem=force_send.at[j],
                recv_sem=force_recv.at[j],
                device_id={"dom": peer},
                device_id_type=MESH,
            )
        )
        force_copies[-1].start()
    result = packed[me]
    for j in range(1, doms):
        force_copies[j - 1].wait_recv()
        result += arrived[j]
    force_ref[...] = result
    for copy in force_copies:
        copy.wait_send()


def body(
    doms,
    grps,
    profile,
    forcing,
    height,
    area,
    stretch,
    face_cell,
    match_owner,
    match_block,
    live_blocks,
    cell_velocity,
):
    blocks, _, points, faces = profile.shape
    rows = 2 * cell_velocity.shape[0]
    everything = pl.BlockSpec(memory_space=pl.ANY)
    vmem = pl.BlockSpec(memory_space=pltpu.VMEM)
    deep = (points, blocks, faces)
    dma = pltpu.SemaphoreType.DMA
    args = (
        profile,
        forcing.astype(F32).reshape(2 * blocks, faces),
        height,
        area,
        stretch.reshape(1, blocks),
        face_cell,
        match_owner,
        match_block,
        live_blocks.reshape(1, -1),
        cell_velocity.reshape(rows, faces),
    )
    shear, force = pl.pallas_call(
        functools.partial(kernel, doms, grps),
        out_shape=(
            jax.ShapeDtypeStruct((2 * blocks, faces), F32),
            jax.ShapeDtypeStruct((rows, faces), F32),
        ),
        in_specs=[everything] * len(args),
        out_specs=(vmem, vmem),
        scratch_shapes=[pltpu.VMEM(arg.shape, arg.dtype) for arg in args[:-1]]
        + [
            pltpu.VMEM((doms, rows, faces), BF16),
            pltpu.VMEM((blocks * 2 * points, faces), F32),
            pltpu.VMEM((points, 2, blocks, faces), F32),
            pltpu.VMEM((points, 2, blocks, faces), F32),
            pltpu.VMEM(deep, F32),
            pltpu.VMEM(deep, F32),
            pltpu.VMEM(deep, F32),
            pltpu.VMEM(deep, F32),
            pltpu.VMEM((blocks, faces, faces), BF16),
            pltpu.VMEM((8 * blocks, faces), F32),
            pltpu.VMEM((doms, rows, faces), F32),
            pltpu.VMEM((doms, rows, faces), F32),
            dma((len(args) - 1,)),
            dma,
            dma((doms,)),
            dma((doms,)),
            dma((doms,)),
            dma((doms,)),
        ],
        compiler_params=pltpu.CompilerParams(collective_id=0, has_side_effects=True),
        name="wall_model",
    )(*args)
    return (
        shear.reshape(blocks, 2, faces),
        force.reshape(cell_velocity.shape[0], 2, faces),
    )


def solution(mesh):
    in_specs = (
        P(("dom", "grp"), None, None, None),
        P(("dom", "grp"), None, None),
        P(("dom", "grp"), None),
        P(("dom", "grp"), None),
        P(("dom", "grp")),
        P(("dom", "grp"), None),
        P(None, "grp", None),
        P(None, "grp", None),
        P(),
        P(("dom", "grp"), None, None),
    )
    out_specs = (P(("dom", "grp"), None, None), P(("dom", "grp"), None, None))
    step = functools.partial(body, mesh.shape["dom"], mesh.shape["grp"])
    return jax.shard_map(step, mesh=mesh, in_specs=in_specs, out_specs=out_specs, check_vma=False)
```

time: 222 us -> 24.5 us (0.11)
  starting transfers between devices: 77.8 us -> 0 us
  local copies, waits for them, and re-layouts: 72.6 us -> 1.96 us
  other arithmetic: 55 us -> 1.32 us
  Pallas kernels: 0 us -> 20.3 us
  waiting for transfers between devices: 6.71 us -> 0 us
  loops' own time: 5.29 us -> 0 us
    all_to_all x2 -> x0, starting transfers between devices: 77.8 us -> none  [the longest x1 70.5 us: body(): lax.all_to_all(packed_force.reshape(dom_count, capacity, 2 * face_count),...]
    gather x3 -> x0, local copies, waits for them, and re-layouts: 55.9 us -> none  [the longest x1 54.6 us: body(): jnp.take_along_axis(slot_rows, jnp.broadcast_to(face_cell[:, None, :], sl...]
    pallas_call x0 -> x1, Pallas kernels: none -> 20.3 us  [body(): pl.pallas_call(functools.partial(kernel, doms, grps), out_shape=(jax.Shap...]
    div x138 -> x0, other arithmetic: 11.9 us -> none  [the longest x132 11.6 us: thomas_solve(): (right_side[:, :, level] - lower_now[:, None] * value_now) / denom[:, None]]
    while x33 -> x0, other arithmetic: 10.6 us -> none
    sub x36 -> x0, other arithmetic: 9.65 us -> none  [the longest x12 6.81 us: thomas_solve(): denom = diagonal[:, level] - lower_now * factor_now]
    while x918 -> x0, local copies, waits for them, and re-layouts: 9.17 us -> none
    select_n x41 -> x0, other arithmetic: 7.42 us -> none  [the longest x12 2.49 us: implicit_step(): lower_band = jnp.where((row_index == 0) | last_row, 0.0, -down_coef)]
  transfers between devices with their start and end apart: 2 -> 0, of which waited for: 2 -> 0; matrix products, arithmetic and copies ran while one was open for 3% -> 0% of each run, Pallas kernels for 0% -> 0%
where the time goes in v1:
time: 24.5 us; the launch traced here: 24.3 us
  Pallas kernels  20.3 us (83%)
  local copies, waits for them, and re-layouts  1.96 us (8%)
  other arithmetic  1.32 us (5%)
  between operations  0.65 us (3%)
    pallas_call x1, Pallas kernels, body(): pl.pallas_call(functools.partial(kernel, doms, grps), out_shape=(jax.Shap...  20.3 us
    unnamed x4, local copies, waits for them, and re-layouts  1.96 us
    reshape x1, other arithmetic, body(): forcing.astype(F32).reshape(2 * blocks, faces)  1.32 us

profile of v1, /device:TPU:0, one launch (start us, length us, event | category | flops | bytes accessed | tf_op | source)
XLA Modules:
  0.0 24.3 jit_solution(5813173499024522745)
XLA Ops:
  0.6 1.3 %convert.1.forc_h = f32[48,128]{1,0:T(8,128)} convert(bf16[48,128]{1,0:T(8,128)(2,1)} %bitcast.9) | non-fusion elementwise | flops 6144 | bytes 36864 | tf_op jit(solution)/shard_map/reshape | solution.py:338
  1.9 20.3 %wall_model.1 = (f32[48,128]{1,0:T(8,128)}, f32[24,128]{1,0:T(8,128)}) custom-call(bf16[24,2,64,128]{3,2,1,0:T(8,128)(2,1)} %prof_h.1, f32[48,128]{1,0:T(8,128)} %convert.1.forc_h, bf16[24,128]{1,0:T(8,128)(2,1)} %height_h.1, f32[24,128]{1,0:T(8,128)} %area_h.1, s32[1,24]{1,0:T(1,128)} %bitcast.11, s32[24,128]{1,0:T(8,128)} %face_h.1, s32[8,1,24]{2,1,0:T(1,128)} %owner_h.1, ...), custom_call_target="tpu_custom_call" | custom-call | tf_op jit(solution)/shard_map/wall_model/pallas_call | solution.py:348
  22.3 0.0 copy-start
  22.3 1.4 %copy.14 = f32[24,2,128]{2,1,0:T(2,128)} copy(f32[24,2,128]{2,1,0:T(2,128)} %bitcast.7) | data formatting | bytes 49152
  23.7 0.0 copy-done
  23.7 0.6 %copy.15 = f32[12,2,128]{2,1,0:T(2,128)} copy(f32[12,2,128]{2,1,0:T(2,128)S(1)} %bitcast.8) | data formatting | bytes 24576
Async XLA Ops:
  22.3 1.4 %copy-start = (f32[24,128]{1,0:T(8,128)S(1)}, f32[24,128]{1,0:T(8,128)}, u32[]{:S(2)}) copy-start(f32[24,128]{1,0:T(8,128)} %get-tuple-element.5) | copy-start | bytes 36868

commit v2 on v1

--- a/solution.py
+++ b/solution.py
@@ -54,6 +54,7 @@
     cells,
     packed,
     arrived,
+    forc32,
     in_sem,
     own_sem,
     cell_send,
@@ -151,6 +152,7 @@
 
     lax.fori_loop(0, points, turn, 0)
 
+    forc32[...] = forc[...].astype(F32)
     face_now = face[...]
     cell_ids = lax.broadcasted_iota(jnp.int32, (faces, faces), 0)
 
@@ -179,7 +181,7 @@
     ]
     source = []
     for c in range(2):
-        push = forc[pl.ds(c, blocks, stride=2), :] + matching[c] - u[points - 1, c]
+        push = forc32[pl.ds(c, blocks, stride=2), :] + matching[c] - u[points - 1, c]
         source.append(TIME_STEP * PUSH_GAIN * push)
         u[points - 1, c] = matching[c]
 
@@ -329,13 +331,14 @@
 ):
     blocks, _, points, faces = profile.shape
     rows = 2 * cell_velocity.shape[0]
-    everything = pl.BlockSpec(memory_space=pl.ANY)
+    everything = pl.BlockSpec(memory_space=pltpu.HBM)
     vmem = pl.BlockSpec(memory_space=pltpu.VMEM)
     deep = (points, blocks, faces)
     dma = pltpu.SemaphoreType.DMA
+    vmem_bytes = 32 << 20
     args = (
         profile,
-        forcing.astype(F32).reshape(2 * blocks, faces),
+        forcing.reshape(2 * blocks, faces),
         height,
         area,
         stretch.reshape(1, blocks),
@@ -367,6 +370,7 @@
             pltpu.VMEM((8 * blocks, faces), F32),
             pltpu.VMEM((doms, rows, faces), F32),
             pltpu.VMEM((doms, rows, faces), F32),
+            pltpu.VMEM((2 * blocks, faces), F32),
             dma((len(args) - 1,)),
             dma,
             dma((doms,)),
@@ -374,9 +378,11 @@
             dma((doms,)),
             dma((doms,)),
         ],
-        compiler_params=pltpu.CompilerParams(collective_id=0, has_side_effects=True),
+        compiler_params=pltpu.CompilerParams(
+            collective_id=0, has_side_effects=True, vmem_limit_bytes=vmem_bytes
+        ),
         name="wall_model",
-    )(*args)
+    )(*[pltpu.with_memory_space_constraint(x, pltpu.HBM) for x in args])
     return (
         shear.reshape(blocks, 2, faces),
         force.reshape(cell_velocity.shape[0], 2, faces),

time: 24.5 us -> 21.8 us (0.89)
  other arithmetic: 1.32 us -> 0 us
  local copies, waits for them, and re-layouts: 1.96 us -> 1.21 us
  Pallas kernels: 20.3 us -> 19.8 us
    reshape x1 -> x0, other arithmetic: 1.32 us -> none  [body(): forcing.astype(F32).reshape(2 * blocks, faces)]
    unnamed x4 -> x2, local copies, waits for them, and re-layouts: 1.96 us -> 1.21 us
    pallas_call x1, Pallas kernels: 20.3 us -> 19.8 us  [body(): pl.pallas_call(functools.partial(kernel, doms, grps), out_shape=(jax.Shap...]
where the time goes in v2:
time: 21.8 us; the launch traced here: 21.6 us
  Pallas kernels  19.8 us (91%)
  local copies, waits for them, and re-layouts  1.21 us (6%)
  between operations  0.64 us (3%)
    pallas_call x1, Pallas kernels, body(): pl.pallas_call(functools.partial(kernel, doms, grps), out_shape=(jax.Shap...  19.8 us
    unnamed x2, local copies, waits for them, and re-layouts  1.21 us

profile of v2, /device:TPU:0, one launch (start us, length us, event | category | flops | bytes accessed | tf_op | source)
XLA Modules:
  0.0 21.6 jit_solution(17780799616881275499)
XLA Ops:
  0.6 19.8 %wall_model.1 = (f32[48,128]{1,0:T(8,128)S(1)}, f32[24,128]{1,0:T(8,128)S(1)}) custom-call(bf16[24,2,64,128]{3,2,1,0:T(8,128)(2,1)} %prof_h.1, bf16[48,128]{1,0:T(8,128)(2,1)} %bitcast.8, bf16[24,128]{1,0:T(8,128)(2,1)} %height_h.1, f32[24,128]{1,0:T(8,128)} %area_h.1, s32[1,24]{1,0:T(1,128)} %bitcast.10, s32[24,128]{1,0:T(8,128)} %face_h.1, ...), custom_call_target="tpu_custom_call" | custom-call | tf_op jit(solution)/shard_map/wall_model/pallas_call | solution.py:351
  20.4 0.6 %copy.14 = f32[24,2,128]{2,1,0:T(2,128)} copy(f32[24,2,128]{2,1,0:T(2,128)S(1)} %bitcast.6) | data formatting | bytes 49152
  21.0 0.6 %copy.15 = f32[12,2,128]{2,1,0:T(2,128)} copy(f32[12,2,128]{2,1,0:T(2,128)S(1)} %bitcast.7) | data formatting | bytes 24576

commit v3 on v2

--- a/solution.py
+++ b/solution.py
@@ -284,13 +284,18 @@
             part, pick[b], (((1,), (1,)), ((), ())), preferred_element_type=F32
         )
     slot_row = lax.broadcasted_iota(jnp.int32, (slots, blocks), 0)
-    total = jnp.zeros((slots, faces), F32)
+    places, terms = [], []
     for c in range(2):
         by_cell = cells[pl.ds(c, blocks, stride=8), :] + cells[pl.ds(2 + c, blocks, stride=8), :]
         place = (slot_row == row_global + c).astype(F32)
-        total += jnp.dot(
-            place, by_cell, precision=lax.Precision.HIGHEST, preferred_element_type=F32
-        )
+        top = by_cell.astype(BF16).astype(F32)
+        places += [place, place]
+        terms += [top, by_cell - top]
+    total = jnp.dot(
+        jnp.concatenate(places, axis=1).astype(BF16),
+        jnp.concatenate(terms, axis=0).astype(BF16),
+        preferred_element_type=F32,
+    )
     packed[...] = total.reshape(doms, rows, faces)
     force_copies = []
     for j in range(1, doms):
@@ -313,6 +318,17 @@
     force_ref[...] = result
     for copy in force_copies:
         copy.wait_send()
+
+
+def emit(shear_ref, force_ref, shear_out, force_out, sem):
+    copies = (
+        pltpu.make_async_copy(shear_ref, shear_out, sem.at[0]),
+        pltpu.make_async_copy(force_ref, force_out, sem.at[1]),
+    )
+    for copy in copies:
+        copy.start()
+    for copy in copies:
+        copy.wait()
 
 
 def body(
@@ -383,6 +399,18 @@
         ),
         name="wall_model",
     )(*[pltpu.with_memory_space_constraint(x, pltpu.HBM) for x in args])
+    shear, force = pl.pallas_call(
+        emit,
+        out_shape=(
+            jax.ShapeDtypeStruct(shear.shape, F32),
+            jax.ShapeDtypeStruct(force.shape, F32),
+        ),
+        in_specs=[pl.BlockSpec(memory_space=pl.ANY)] * 2,
+        out_specs=(pl.BlockSpec(memory_space=pl.ANY),) * 2,
+        scratch_shapes=[dma((2,))],
+        compiler_params=pltpu.CompilerParams(vmem_limit_bytes=1 << 20),
+        name="emit",
+    )(shear, force)
     return (
         shear.reshape(blocks, 2, faces),
         force.reshape(cell_velocity.shape[0], 2, faces),

time: 21.8 us -> 20.8 us (0.954)
  local copies, waits for them, and re-layouts: 1.21 us -> 0 us
    unnamed x2 -> x0, local copies, waits for them, and re-layouts: 1.21 us -> none
    pallas_call x0 -> x1, Pallas kernels: none -> 0.63 us  [body(): pl.pallas_call(emit, out_shape=(jax.ShapeDtypeStruct(shear.shape, F32), j...]
    pallas_call x1, Pallas kernels: 19.8 us -> 19.4 us  [body(): pl.pallas_call(functools.partial(kernel, doms, grps), out_shape=(jax.Shap...]
where the time goes in v3:
time: 20.8 us; the launch traced here: 20.6 us
  Pallas kernels  20 us (96%)
  between operations  0.64 us (3%)
    pallas_call x1, Pallas kernels, body(): pl.pallas_call(functools.partial(kernel, doms, grps), out_shape=(jax.Shap...  19.4 us
    pallas_call x1, Pallas kernels, body(): pl.pallas_call(emit, out_shape=(jax.ShapeDtypeStruct(shear.shape, F32), j...  0.63 us

profile of v3, /device:TPU:0, one launch (start us, length us, event | category | flops | bytes accessed | tf_op | source)
XLA Modules:
  0.0 20.6 jit_solution(15907645907133630200)
XLA Ops:
  0.6 19.4 %wall_model.1 = (f32[48,128]{1,0:T(8,128)S(1)}, f32[24,128]{1,0:T(8,128)S(1)}) custom-call(bf16[24,2,64,128]{3,2,1,0:T(8,128)(2,1)} %prof_h.1, bf16[48,128]{1,0:T(8,128)(2,1)} %bitcast.6, bf16[24,128]{1,0:T(8,128)(2,1)} %height_h.1, f32[24,128]{1,0:T(8,128)} %area_h.1, s32[1,24]{1,0:T(1,128)} %bitcast.8, s32[24,128]{1,0:T(8,128)} %face_h.1, ...), custom_call_target="tpu_custom_call" | custom-call | tf_op jit(solution)/shard_map/wall_model/pallas_call | solution.py:367
  20.0 0.6 %emit.1 = (f32[48,128]{1,0:T(8,128)}, f32[24,128]{1,0:T(8,128)}) custom-call(f32[48,128]{1,0:T(8,128)S(1)} %get-tuple-element.6.shear_ref, f32[24,128]{1,0:T(8,128)S(1)} %get-tuple-element.7.force_ref), custom_call_target="tpu_custom_call" | custom-call | tf_op jit(solution)/shard_map/emit/pallas_call | solution.py:402
